TPU v7x, 512 devices: a whole 4x8x8 slice. The times are simulated.
512 devices in a mesh: wide: 32 (over y, z_lo, core), narrow: 16 (over z_hi, x).
Axes of the slice: x: 4, y: 8, z: 8 (z_hi: 4, z_lo: 2; z = z_hi * 2 + z_lo), core: 2. Of those that a mesh axis runs over, the one named last changes fastest.
Arguments:
- beams: bfloat16 [128, 256, 256], P('narrow'), may hold values from -0.375 to 0.375
- basis: bfloat16 [32768, 128], P('wide'), may hold values from -0.375 to 0.375
- foreground: float32 [128, 128, 256], P('narrow', 'wide'), may hold values from 0.3 to 3
- signal: float32 [128, 128, 256], P('narrow', 'wide'), may hold values from 0.3 to 3
- band_start: int32 [128], P('narrow'), may hold values from 0 to 96, as said below
- band_width: int32 [128], P('narrow'), may hold values from 32 to 128
Outputs:
- projected_rows: float32 [32768, 128], P(('wide', 'narrow'))
- kl_matrix: float32 [128, 128], replicated
Inputs may be any that keep to these rules, and one draw needn't show every extreme that they name: band_start + band_width <= 128 in every block row.
All inputs are finite; a program needn't handle non-finite values.
Results may differ from a plain program's by a relative error of at most 0.0041.
Values may be sent and summed in bfloat16 or wider, within the bound.
A program may use at most 64 MiB of HBM per device.

v0:
```python
import jax
import jax.numpy as jnp
from jax import lax
from jax.sharding import PartitionSpec as P

NFREQ = 128


def spread(value, axis, source):
    kept = jnp.where(lax.axis_index(axis) == source, value, 0).astype(value.dtype)
    return lax.psum(kept, axis)


def per_device(beams, basis, foreground, signal, band_start, band_width):
    row_index = lax.axis_index("narrow")
    col_index = lax.axis_index("wide")
    row_freqs = beams.shape[0]
    col_freqs = foreground.shape[1]
    nbeam = beams.shape[1]
    factor = row_freqs // col_freqs
    own_slice = lax.dynamic_slice_in_dim(beams, col_index % factor * col_freqs, col_freqs, 0)
    col_beams = spread(own_slice, "narrow", col_index // factor)
    whole = lax.all_gather(basis, "wide", axis=0, tiled=True)
    row_basis = lax.dynamic_slice_in_dim(whole, row_index * row_freqs * nbeam, row_freqs * nbeam, 0)
    row_basis = row_basis.reshape(row_freqs, nbeam, basis.shape[1])
    col_global = col_index * col_freqs + jnp.arange(col_freqs, dtype=jnp.int32)
    lower = band_start[:, None]
    inband = (
        (col_global[None, :] >= lower) & (col_global[None, :] < lower + band_width[:, None])
    ).astype(jnp.float32)
    columns = []
    for column in range(col_freqs):
        spectrum = foreground[:, column, :] + inband[:, column][:, None] * signal[:, column, :]
        scaled = (beams * spectrum[:, None, :]).astype(jnp.bfloat16)
        block = jnp.einsum(
            "fbl,cl->fbc", scaled, col_beams[column], preferred_element_type=jnp.float32
        ).astype(jnp.bfloat16)
        columns.append(
            jnp.einsum("fbc,fbk->ck", block, row_basis, preferred_element_type=jnp.float32)
        )
    partial_rows = jnp.concatenate(columns, axis=0)
    projected = lax.psum_scatter(partial_rows, "narrow", scatter_dimension=0, tiled=True)
    count = projected.shape[0]
    local_basis = lax.dynamic_slice_in_dim(basis, row_index * count, count, 0)
    term = jnp.dot(
        projected.T,
        local_basis.astype(jnp.float32),
        precision=lax.Precision.HIGH,
        preferred_element_type=jnp.float32,
    )
    kl_matrix = lax.psum(term, ("wide", "narrow")) / NFREQ
    return (projected, kl_matrix)


def solution(mesh):
    placed = (
        P("narrow", None, None),
        P("wide", None),
        P("narrow", "wide", None),
        P("narrow", "wide", None),
        P("narrow"),
        P("narrow"),
    )
    return jax.shard_map(
        per_device,
        mesh=mesh,
        in_specs=placed,
        out_specs=(P(("wide", "narrow"), None), P()),
        check_vma=False,
    )
```

profile of v0, /device:TPU:1, one launch (start us, length us, event | category | flops | bytes accessed | tf_op | source)
XLA Modules:
  0.0 558.6 jit_solution(6742256649662964978)
XLA Ops:
  8.0 0.0 copy-start
  8.0 0.0 all-gather.2.cloned.1.call-start
  8.1 0.7 all-gather.2.cloned.1.call-update
  8.7 0.0 all-reduce.3.cloned.1.call-start
  8.8 1.9 dynamic-slice_select_fusion
  10.8 0.0 all-reduce.3.cloned.1.call-update
  10.8 0.0 reduce-scatter.2.cloned.1.call-start
  10.8 0.9 fusion.40
  11.8 0.9 fusion.39
  12.7 0.7 add.52
  13.4 0.7 and_convert_fusion
  14.1 0.1 fusion.31
  14.2 0.1 fusion.35
  14.3 78.3 %all-gather.2.cloned.1.call-done = bf16[32768,128]{1,0:T(8,128)(2,1)} async-done(((bf16[1024,128]{1,0:T(8,128)(2,1)}), bf16[32768,128]{1,0:T(8,128)(2,1)}) %all-gather.2.cloned.1.call-update) | async-done | bytes 8388624 | tf_op jit(solution)/shard_map/all_gather | solution.py:23
  92.6 1.1 constant_dynamic-slice_fusion
  93.7 88.7 %all-reduce.3.cloned.1.call-done = bf16[4,256,256]{2,1,0:T(8,128)(2,1)} async-done(((bf16[4,256,256]{2,1,0:T(8,128)(2,1)}), bf16[4,256,256]{2,1,0:T(8,128)(2,1)}) %all-reduce.3.cloned.1.call-update) | async-done | bytes 524304 | tf_op jit(solution)/shard_map/psum | solution.py:11
  182.3 0.0 copy-start.1
  182.3 0.0 copy-done
  182.3 1.7 fusion.8
  184.1 0.0 copy-done.1
  184.1 0.8 fusion.9
  184.8 0.8 fusion.10
  185.6 0.8 fusion.11
  186.4 0.8 pad_maximum_fusion
  187.2 0.0 reduce-scatter.2.cloned.1.call-update
  187.2 0.0 all-reduce.5.cloned.1.call-start
  187.3 98.4 %reduce-scatter.2.cloned.1.call-done = f32[64,128]{1,0:T(8,128)} async-done(((f32[1024,128]{1,0:T(8,128)}), f32[64,128]{1,0:T(8,128)}) %reduce-scatter.2.cloned.1.call-update) | async-done | bytes 32784 | tf_op jit(solution)/shard_map/reduce_scatter | solution.py:42
  285.7 1.6 fusion.28
  287.3 0.0 all-reduce.5.cloned.1.call-update
  287.3 262.3 %all-reduce.5.cloned.1.call-done = f32[128,128]{1,0:T(8,128)} async-done(((f32[128,128]{1,0:T(8,128)}), f32[128,128]{1,0:T(8,128)}) %all-reduce.5.cloned.1.call-update) | async-done | bytes 65552 | tf_op jit(solution)/shard_map/psum | solution.py:51
  549.6 1.5 broadcast_multiply_fusion
  (2 shorter events, 0.0 us)
Async XLA Ops:
  8.0 174.3 %copy-start = (bf16[8,256,256]{2,1,0:T(8,128)(2,1)S(1)}, bf16[8,256,256]{2,1,0:T(8,128)(2,1)}, u32[]{:S(2)}) copy-start(bf16[8,256,256]{2,1,0:T(8,128)(2,1)} %param.6) | copy-start | bytes 3145732
  8.0 84.6 %all-gather.2.cloned.1.call-start = ((), (), s32[]{:S(2)}) async-start(), calls=%async_computation.2 | async-start | bytes 8650752 | tf_op jit(solution)/shard_map/all_gather | solution.py:23
  8.7 173.6 %all-reduce.3.cloned.1.call-start = ((), (), s32[]{:S(2)}) async-start(), calls=%async_computation.1 | async-start | bytes 1048576 | tf_op jit(solution)/shard_map/psum | solution.py:11
  10.8 274.9 %reduce-scatter.2.cloned.1.call-start = ((), (), s32[]{:S(2)}) async-start(), calls=%async_computation.3 | async-start | bytes 557056 | tf_op jit(solution)/shard_map/reduce_scatter | solution.py:42
  182.3 1.7 copy-start.1
  187.2 362.4 %all-reduce.5.cloned.1.call-start = ((), (), s32[]{:S(2)}) async-start(), calls=%async_computation.4 | async-start | bytes 131072 | tf_op jit(solution)/shard_map/psum | solution.py:51
Sparse Core Ops, SparseCore 0:
  11.2 81.3 all-gather.1
Sparse Core Ops, SparseCore 1:
  12.1 170.1 all-reduce.2
  187.4 98.3 reduce-scatter.1
  291.1 258.4 all-reduce.4
where the time goes:
time: 559 us
  waiting for transfers between devices  528 us (94%)
  between operations  15.8 us (3%)
  other arithmetic  5.79 us (1%)
  matrix products  5.61 us (1%)
    psum x1, waiting for transfers between devices, per_device(): kl_matrix = lax.psum(term, ('wide', 'narrow')) / NFREQ  262 us
    reduce_scatter x1, waiting for transfers between devices, per_device(): lax.psum_scatter(partial_rows, 'narrow', scatter_dimension=0, tiled=True)  98.4 us
    psum x1, waiting for transfers between devices, spread(): return lax.psum(kept, axis)  88.7 us
    all_gather x1, waiting for transfers between devices, per_device(): whole = lax.all_gather(basis, 'wide', axis=0, tiled=True)  78.3 us
  transfers between devices with their start and end apart: 4, of which 4 were waited for; matrix products, arithmetic and copies ran while one was open for 1% of the time, Pallas kernels for 0%

commit v1 on v0

v1 whole, which is shorter than its diff:
```python
import jax
import jax.numpy as jnp
from jax import lax
from jax.experimental import pallas as pl
from jax.experimental.pallas import tpu as pltpu
from jax.sharding import PartitionSpec as P

MESH = pl.DeviceIdType.MESH
F32 = jnp.float32
BF16 = jnp.bfloat16
NT = (((1,), (1,)), ((), ()))


def nt(a, b):
    return lax.dot_general(a, b, NT, preferred_element_type=F32)


def split(value):
    high = value.astype(BF16)
    return high, (value - high.astype(F32)).astype(BF16)


def put(src, dst, send, recv, device):
    return pltpu.make_async_remote_copy(
        src_ref=src, dst_ref=dst, send_sem=send, recv_sem=recv, device_id=device, device_id_type=MESH
    )


def drain(ref, sem):
    pltpu.make_async_copy(ref, ref, sem).wait()


def kernel(
    beams_hbm, basis_hbm, fore_hbm, sig_hbm, start_ref, width_ref, proj_ref, kl_ref,
    beams_v, basis_v, fore_v, sig_v, basis_t, basis_in, beam_in, spec, part, got, mine, rows, term, got5, own6, got6, kl_v,
    local, send, recv,
):
    w = lax.axis_index("wide")
    n = lax.axis_index("narrow")
    y, q = lax.div(w, 4), lax.rem(w, 4)
    z, x = lax.div(n, 4), lax.rem(n, 4)
    chip, core = lax.div(w, 2), lax.rem(w, 2)
    g = x * 4 + q
    h = y * 4 + z
    diagonal = chip == n

    load_basis = pltpu.make_async_copy(basis_hbm, basis_v, local.at[0])
    load_fore = pltpu.make_async_copy(fore_hbm, fore_v, local.at[1])
    load_sig = pltpu.make_async_copy(sig_hbm, sig_v, local.at[2])
    load_beams = pltpu.make_async_copy(beams_hbm, beams_v, local.at[3])
    load_basis.start()
    load_fore.start()
    load_sig.start()
    load_beams.start()

    def in_narrow(i):
        other = lax.rem(n + i, 16)
        return other, (w, other)

    def in_group(i):
        other = lax.rem(g + i, 16)
        return other, (y * 4 + lax.rem(other, 4), z * 4 + lax.div(other, 4))

    def in_rest(i):
        other = lax.rem(h + i, 32)
        return other, (lax.div(other, 4) * 4 + q, lax.rem(other, 4) * 4 + x)

    barrier = pltpu.get_barrier_semaphore()

    def greet(device):
        pl.semaphore_signal(barrier, inc=1, device_id=device, device_id_type=MESH)

    @pl.loop(1, 16)
    def _(i):
        greet(in_narrow(i)[1])
        greet(in_group(i)[1])

    @pl.loop(1, 32)
    def _(i):
        greet(in_rest(i)[1])

    greet((2 * n + 1 - core, chip))

    @pl.when(jnp.logical_not(diagonal))
    def _():
        greet((2 * n + core, chip))

    load_fore.wait()
    load_sig.wait()
    column = 4 * w + lax.broadcasted_iota(jnp.int32, (4, 256), 0)
    for f in range(8):
        low = start_ref[f]
        inband = ((column >= low) & (column < low + width_ref[f])).astype(F32)
        spec[q, pl.ds(4 * f, 4), :] = fore_v[f] + inband * sig_v[f]
    load_basis.wait()
    for f in range(4):
        basis_t[f] = basis_v[pl.ds(256 * f, 256), :].astype(F32).T.astype(BF16)
    load_beams.wait()

    pl.semaphore_wait(barrier, 63 - diagonal.astype(jnp.int32))

    for i in range(1, 4):
        put(spec.at[q], spec.at[q], send.at[0], recv.at[0], (y * 4 + lax.rem(q + i, 4), n)).start()
    far_half = 2 * lax.rem(n, 2)
    beam_src = beams_v.at[4 * core + lax.div(chip, 4), pl.ds(64 * lax.rem(chip, 4), 64), :]

    def basis_src(to_core):
        return basis_t.at[:, pl.ds(32 * (far_half + to_core), 32), :]

    put(basis_src(1 - core), basis_in.at[core], send.at[1], recv.at[1], (2 * n + 1 - core, chip)).start()

    @pl.when(diagonal)
    def _():
        pltpu.make_async_copy(basis_src(core), basis_in.at[core], recv.at[1]).start()
        pltpu.make_async_copy(beam_src, beam_in, recv.at[2]).start()

    @pl.when(jnp.logical_not(diagonal))
    def _():
        put(basis_src(core), basis_in.at[core], send.at[2], recv.at[1], (2 * n + core, chip)).start()
        put(beam_src, beam_in, send.at[3], recv.at[2], (2 * n + core, chip)).start()

    drain(spec.at[pl.ds(0, 3)], recv.at[0])
    drain(basis_in, recv.at[1])

    made = [
        jnp.dot(basis_in[f // 4, f % 4], beams_v[f], preferred_element_type=F32) for f in range(8)
    ]
    for j in range(4):
        for pair in range(2):
            halves = []
            for r in range(2 * pair, 2 * pair + 2):
                total = spec[r, pl.ds(j, 1), :] * made[0]
                for f in range(1, 8):
                    total = total + spec[r, pl.ds(4 * f + j, 1), :] * made[f]
                halves.append(total)
            for xx in range(4):
                piece = jnp.concatenate([half[8 * xx : 8 * xx + 8] for half in halves], axis=0)
                part[4 * j + xx, pl.ds(16 * pair, 16), :] = piece.astype(BF16)

    @pl.loop(1, 16)
    def _(i):
        other, device = in_narrow(i)
        put(part.at[other], got.at[n], send.at[4], recv.at[3], device).start()

    got[n] = part[n]
    drain(got.at[pl.ds(0, 15)], recv.at[3])
    total = got[0].astype(F32)
    for i in range(1, 16):
        total = total + got[i].astype(F32)
    mine[...] = total

    place = pl.multiple_of(32 * q + 8 * x, 8)

    @pl.loop(1, 16)
    def _(i):
        other, device = in_group(i)
        source = mine.at[pl.ds(pl.multiple_of(8 * lax.rem(other, 4), 8), 8), :]
        put(source, rows.at[pl.ds(place, 8), :], send.at[5], recv.at[4], device).start()

    rows[pl.ds(place, 8), :] = mine[pl.ds(pl.multiple_of(8 * q, 8), 8), :]
    drain(beam_in, recv.at[2])
    drain(rows.at[pl.ds(0, 120)], recv.at[4])

    high, low = split(rows[...])
    chunk = beam_in[...]
    turned = nt(high, chunk) + nt(low, chunk)
    local_basis = basis_v[pl.ds(pl.multiple_of(64 * n, 64), 64), :]
    turned_high, turned_low = split(turned)
    term[...] = jnp.dot(turned_high, local_basis, preferred_element_type=F32) + jnp.dot(
        turned_low, local_basis, preferred_element_type=F32
    )

    @pl.loop(1, 16)
    def _(i):
        other, device = in_group(i)
        source = term.at[pl.ds(pl.multiple_of(8 * other, 8), 8), :]
        put(source, got5.at[g], send.at[6], recv.at[5], device).start()

    got5[g] = term[pl.ds(pl.multiple_of(8 * g, 8), 8), :]
    proj_ref[...] = nt(chunk, high) + nt(chunk, low)
    drain(got5.at[pl.ds(0, 15)], recv.at[5])
    total = got5[0]
    for i in range(1, 16):
        total = total + got5[i]
    own6[...] = total

    @pl.loop(1, 32)
    def _(i):
        other, device = in_rest(i)
        put(own6, got6.at[h], send.at[7], recv.at[6], device).start()

    got6[h] = total
    drain(got6.at[pl.ds(0, 31)], recv.at[6])
    total = got6[0]
    for i in range(1, 32):
        total = total + got6[i]
    here = kl_v.at[pl.ds(pl.multiple_of(8 * g, 8), 8), :]
    here[...] = total * (1.0 / 128)

    @pl.loop(1, 16)
    def _(i):
        other, device = in_group(i)
        put(here, here, send.at[8], recv.at[7], device).start()

    drain(kl_v.at[pl.ds(0, 120)], recv.at[7])
    kl_ref[...] = kl_v[...]

    drain(spec.at[pl.ds(0, 3)], send.at[0])
    drain(basis_in.at[0], send.at[1])

    @pl.when(jnp.logical_not(diagonal))
    def _():
        drain(basis_in.at[0], send.at[2])
        drain(beam_in, send.at[3])

    drain(got.at[pl.ds(0, 15)], send.at[4])
    drain(rows.at[pl.ds(0, 120)], send.at[5])
    drain(got5.at[pl.ds(0, 15)], send.at[6])
    drain(got6.at[pl.ds(0, 31)], send.at[7])
    drain(kl_v.at[pl.ds(0, 120)], send.at[8])


def per_device(beams, basis, foreground, signal, band_start, band_width):
    anywhere = pl.BlockSpec(memory_space=pl.ANY)
    scalars = pl.BlockSpec(memory_space=pltpu.SMEM)
    vector = pl.BlockSpec(memory_space=pltpu.VMEM)
    return pl.pallas_call(
        kernel,
        out_shape=(
            jax.ShapeDtypeStruct((64, 128), F32),
            jax.ShapeDtypeStruct((128, 128), F32),
        ),
        in_specs=[anywhere] * 4 + [scalars] * 2,
        out_specs=(vector, vector),
        scratch_shapes=[
            pltpu.VMEM((8, 256, 256), BF16),
            pltpu.VMEM((1024, 128), BF16),
            pltpu.VMEM((8, 4, 256), F32),
            pltpu.VMEM((8, 4, 256), F32),
            pltpu.VMEM((4, 128, 256), BF16),
            pltpu.VMEM((2, 4, 32, 256), BF16),
            pltpu.VMEM((64, 256), BF16),
            pltpu.VMEM((4, 32, 256), F32),
            pltpu.VMEM((16, 32, 256), BF16),
            pltpu.VMEM((16, 32, 256), BF16),
            pltpu.VMEM((32, 256), F32),
            pltpu.VMEM((128, 256), F32),
            pltpu.VMEM((128, 128), F32),
            pltpu.VMEM((16, 8, 128), F32),
            pltpu.VMEM((8, 128), F32),
            pltpu.VMEM((32, 8, 128), F32),
            pltpu.VMEM((128, 128), F32),
            pltpu.SemaphoreType.DMA((4,)),
            pltpu.SemaphoreType.DMA((9,)),
            pltpu.SemaphoreType.DMA((8,)),
        ],
        compiler_params=pltpu.CompilerParams(
            collective_id=0, has_side_effects=True, vmem_limit_bytes=32 << 20
        ),
    )(beams, basis, foreground, signal, band_start, band_width)


def solution(mesh):
    placed = (
        P("narrow", None, None),
        P("wide", None),
        P("narrow", "wide", None),
        P("narrow", "wide", None),
        P("narrow"),
        P("narrow"),
    )
    return jax.shard_map(
        per_device,
        mesh=mesh,
        in_specs=placed,
        out_specs=(P(("wide", "narrow"), None), P()),
        check_vma=False,
    )
```

time: 559 us -> 88 us (0.16)
  waiting for transfers between devices: 528 us -> 0 us
  Pallas kernels: 0 us -> 80.7 us
  between operations: 15.8 us -> 0.65 us
  other arithmetic: 5.79 us -> 0 us
  matrix products: 5.61 us -> 0 us
    psum x2 -> x0, waiting for transfers between devices: 351 us -> none  [the longest x1 262 us: per_device(): kl_matrix = lax.psum(term, ('wide', 'narrow')) / NFREQ]
    reduce_scatter x1 -> x0, waiting for transfers between devices: 98.4 us -> none  [per_device(): lax.psum_scatter(partial_rows, 'narrow', scatter_dimension=0, tiled=True)]
    pallas_call x0 -> x1, Pallas kernels: none -> 80.7 us  [per_device(): pl.pallas_call(kernel, out_shape=(jax.ShapeDtypeStruct((64, 128), F32), j...]
    all_gather x1 -> x0, waiting for transfers between devices: 78.3 us -> none  [per_device(): whole = lax.all_gather(basis, 'wide', axis=0, tiled=True)]
    unnamed x4 -> x14, local copies, waits for them, and re-layouts: 0.01 us -> 6.24 us
    dot_general x5 -> x0, matrix products: 5.61 us -> none  [the longest x4 4.01 us: per_device(): jnp.einsum('fbc,fbk->ck', block, row_basis, preferred_element_type=jnp.fl...]
  transfers between devices with their start and end apart: 4 -> 0, of which waited for: 4 -> 0; matrix products, arithmetic and copies ran while one was open for 1% -> 0% of each run, Pallas kernels for 0% -> 0%
where the time goes in v1:
time: 88 us; the launch traced here: 87.6 us
  Pallas kernels  80.7 us (92%)
  local copies, waits for them, and re-layouts  6.24 us (7%)
    pallas_call x1, Pallas kernels, per_device(): pl.pallas_call(kernel, out_shape=(jax.ShapeDtypeStruct((64, 128), F32), j...  80.7 us
    unnamed x14, local copies, waits for them, and re-layouts  6.24 us

profile of v1, /device:TPU:1, one launch (start us, length us, event | category | flops | bytes accessed | tf_op | source)
XLA Modules:
  0.0 87.6 jit_solution(14954239180086967731)
XLA Ops:
  0.6 0.0 copy-start
  0.6 1.2 %copy-done = bf16[8,256,256]{2,1,0:T(8,128)(2,1)S(1)} copy-done((bf16[8,256,256]{2,1,0:T(8,128)(2,1)S(1)}, bf16[8,256,256]{2,1,0:T(8,128)(2,1)}, u32[]{:S(2)}) %copy-start) | copy-done | bytes 1048600
  1.9 0.0 copy-start.1
  1.9 0.9 %copy-done.1 = bf16[1024,128]{1,0:T(8,128)(2,1)S(1)} copy-done((bf16[1024,128]{1,0:T(8,128)(2,1)S(1)}, bf16[1024,128]{1,0:T(8,128)(2,1)}, u32[]{:S(2)}) %copy-start.1) | copy-done | bytes 262168
  2.8 0.0 copy-start.2
  2.8 0.8 copy-done.2
  3.6 0.0 copy-start.3
  3.6 0.8 copy-done.3
  4.3 0.0 copy-start.4
  4.3 0.7 copy-done.4
  5.0 0.0 copy-start.5
  5.0 0.7 copy-done.5
  5.6 80.7 %shard_map.77 = (f32[64,128]{1,0:T(8,128)S(1)}, f32[128,128]{1,0:T(8,128)S(1)}) custom-call(bf16[8,256,256]{2,1,0:T(8,128)(2,1)S(1)} %copy-done, bf16[1024,128]{1,0:T(8,128)(2,1)S(1)} %copy-done.1, f32[8,4,256]{2,1,0:T(4,128)S(1)} %copy-done.2, f32[8,4,256]{2,1,0:T(4,128)S(1)} %copy-done.3, s32[8]{0:T(128)S(1)} %copy-done.4, s32[8]{0:T(128)S(1)} %copy-done.5), custom_call_target="tpu_custom_call" | custom-call | tf_op jit(solution)/shard_map/pallas_call | solution.py:227
  86.4 0.6 copy.10
  87.0 0.6 copy.11
Async XLA Ops:
  0.6 1.2 %copy-start = (bf16[8,256,256]{2,1,0:T(8,128)(2,1)S(1)}, bf16[8,256,256]{2,1,0:T(8,128)(2,1)}, u32[]{:S(2)}) copy-start(bf16[8,256,256]{2,1,0:T(8,128)(2,1)} %beams_hbm.1) | copy-start | bytes 3145732
  1.9 0.9 %copy-start.1 = (bf16[1024,128]{1,0:T(8,128)(2,1)S(1)}, bf16[1024,128]{1,0:T(8,128)(2,1)}, u32[]{:S(2)}) copy-start(bf16[1024,128]{1,0:T(8,128)(2,1)} %basis_hbm.1) | copy-start | bytes 786436
  2.8 0.8 copy-start.2
  3.6 0.8 copy-start.3
  4.3 0.7 copy-start.4
  5.0 0.7 copy-start.5

commit v2 on v1

v2 whole, which is shorter than its diff:
```python
import jax
import jax.numpy as jnp
from jax import lax
from jax.experimental import pallas as pl
from jax.experimental.pallas import tpu as pltpu
from jax.sharding import PartitionSpec as P

MESH = pl.DeviceIdType.MESH
F32 = jnp.float32
BF16 = jnp.bfloat16
NT = (((1,), (1,)), ((), ()))


def nt(a, b):
    return lax.dot_general(a, b, NT, preferred_element_type=F32)


def split(value):
    high = value.astype(BF16)
    return high, (value - high.astype(F32)).astype(BF16)


def put(src, dst, send, recv, device):
    return pltpu.make_async_remote_copy(
        src_ref=src, dst_ref=dst, send_sem=send, recv_sem=recv, device_id=device, device_id_type=MESH
    )


def drain(ref, sem):
    pltpu.make_async_copy(ref, ref, sem).wait()


def kernel(
    beams_hbm, basis_hbm, fore_hbm, sig_hbm, start_ref, width_ref, proj_ref, kl_ref,
    beam_v, block_v, basis_v, fore_v, sig_v, basis_t, basis_in, made, beam_in, spec, part, got, mine, rows, term,
    got5, got6, got7, kl_v, local, send, recv,
):
    w = lax.axis_index("wide")
    n = lax.axis_index("narrow")
    y, q = lax.div(w, 4), lax.rem(w, 4)
    z, x = lax.div(n, 4), lax.rem(n, 4)
    chip, core = lax.div(w, 2), lax.rem(w, 2)
    g = x * 4 + q

    to_f = lax.rem(z - lax.div(chip, 4) + 4, 4)
    to_y = 4 * core + to_f
    to_q = lax.rem(x - lax.rem(chip, 4) - core + 9, 4)
    turn = lax.rem(y - lax.div(n, 2) + 8, 8)
    to_core, to_z = lax.rem(turn, 2), lax.div(turn, 2)
    to_x = 2 * lax.rem(q, 2) + 1 - lax.div(q, 2)
    basis_target = (4 * to_y + to_q, chip)
    beam_target = (2 * n + to_core, 4 * to_z + to_x)
    high_y = lax.div(y, 4)
    basis_source = (2 * n + high_y, 4 * lax.rem(y + z, 4) + lax.rem(q + high_y + 3 + x, 4))
    beam_source = (4 * lax.rem(y + 2 * z + core, 8) + 2 * (1 - lax.rem(x, 2)) + lax.div(x, 2), chip)

    load_block = pltpu.make_async_copy(
        basis_hbm.at[pl.ds(pl.multiple_of(256 * to_f, 256), 256), :], block_v, local.at[0]
    )
    load_fore = pltpu.make_async_copy(fore_hbm, fore_v, local.at[1])
    load_sig = pltpu.make_async_copy(sig_hbm, sig_v, local.at[2])
    load_beam = pltpu.make_async_copy(beams_hbm.at[y], beam_v, local.at[3])
    load_basis = pltpu.make_async_copy(
        basis_hbm.at[pl.ds(pl.multiple_of(64 * n, 64), 64), :], basis_v, local.at[4]
    )
    load_block.start()
    load_fore.start()
    load_sig.start()
    load_beam.start()
    load_basis.start()

    def in_narrow(i):
        other = lax.rem(n + i, 16)
        return other, (w, other)

    def in_group(i):
        other = lax.rem(g + i, 16)
        return other, (y * 4 + lax.rem(other, 4), z * 4 + lax.div(other, 4))

    def in_y(i):
        return (4 * lax.rem(y + i, 8) + q, n)

    def in_z(i):
        return (w, 4 * lax.rem(z + i, 4) + x)

    barrier = pltpu.get_barrier_semaphore()

    def greet(device):
        pl.semaphore_signal(barrier, inc=1, device_id=device, device_id_type=MESH)

    greet(basis_source)
    greet(beam_source)

    @pl.loop(1, 16)
    def _(i):
        greet(in_group(i)[1])
        greet(in_narrow(i)[1])

    @pl.loop(1, 8)
    def _(i):
        greet(in_y(i))

    load_fore.wait()
    load_sig.wait()
    column = 4 * w + lax.broadcasted_iota(jnp.int32, (4, 256), 0)
    for f in range(8):
        low = start_ref[f]
        inband = ((column >= low) & (column < low + width_ref[f])).astype(F32)
        spec[q, pl.ds(4 * f, 4), :] = fore_v[f] + inband * sig_v[f]
    load_block.wait()
    basis_t[...] = block_v[...].astype(F32).T.astype(BF16)

    pl.semaphore_wait(barrier, 39)

    columns = basis_t.at[pl.ds(pl.multiple_of(32 * to_q, 32), 32), :]
    put(columns, basis_in, send.at[1], recv.at[1], basis_target).start()
    for i in range(1, 4):
        put(spec.at[q], spec.at[q], send.at[0], recv.at[0], (y * 4 + lax.rem(q + i, 4), n)).start()
    chunk_rows = pl.ds(pl.multiple_of(64 * to_x, 64), 64)
    put(beams_hbm.at[4 * to_core + to_z, chunk_rows, :], beam_in, send.at[2], recv.at[2], beam_target).start()

    load_beam.wait()
    drain(basis_in, recv.at[1])
    made[y] = jnp.dot(basis_in[...], beam_v[...], preferred_element_type=F32).astype(BF16)

    for i in range(1, 8):
        put(made.at[y], made.at[y], send.at[3], recv.at[8], in_y(i)).start()
    drain(spec.at[pl.ds(0, 3)], recv.at[0])
    drain(made.at[pl.ds(0, 7)], recv.at[8])

    wide_made = [made[f].astype(F32) for f in range(8)]
    for j in range(4):
        for pair in range(2):
            halves = []
            for r in range(2 * pair, 2 * pair + 2):
                total = spec[r, pl.ds(j, 1), :] * wide_made[0]
                for f in range(1, 8):
                    total = total + spec[r, pl.ds(4 * f + j, 1), :] * wide_made[f]
                halves.append(total)
            for xx in range(4):
                piece = jnp.concatenate([half[8 * xx : 8 * xx + 8] for half in halves], axis=0)
                part[4 * j + xx, pl.ds(16 * pair, 16), :] = piece.astype(BF16)

    @pl.loop(1, 16)
    def _(i):
        other, device = in_narrow(i)
        put(part.at[other], got.at[n], send.at[4], recv.at[3], device).start()

    got[n] = part[n]
    drain(got.at[pl.ds(0, 15)], recv.at[3])
    total = got[0].astype(F32)
    for i in range(1, 16):
        total = total + got[i].astype(F32)
    mine[...] = total

    place = pl.multiple_of(32 * q + 8 * x, 8)

    @pl.loop(1, 16)
    def _(i):
        other, device = in_group(i)
        source = mine.at[pl.ds(pl.multiple_of(8 * lax.rem(other, 4), 8), 8), :]
        put(source, rows.at[pl.ds(place, 8), :], send.at[5], recv.at[4], device).start()

    rows[pl.ds(place, 8), :] = mine[pl.ds(pl.multiple_of(8 * q, 8), 8), :]
    drain(beam_in, recv.at[2])
    drain(rows.at[pl.ds(0, 120)], recv.at[4])

    high, low = split(rows[...])
    chunk = beam_in[...]
    turned = nt(high, chunk) + nt(low, chunk)
    load_basis.wait()
    local_basis = basis_v[...]
    turned_high, turned_low = split(turned)
    term[...] = jnp.dot(turned_high, local_basis, preferred_element_type=F32) + jnp.dot(
        turned_low, local_basis, preferred_element_type=F32
    )

    @pl.loop(1, 16)
    def _(i):
        other, device = in_group(i)
        source = term.at[pl.ds(pl.multiple_of(8 * other, 8), 8), :]
        put(source, got5.at[g], send.at[6], recv.at[5], device).start()

    got5[g] = term[pl.ds(pl.multiple_of(8 * g, 8), 8), :]
    proj_ref[...] = nt(chunk, high) + nt(chunk, low)
    drain(got5.at[pl.ds(0, 15)], recv.at[5])
    total = got5[0]
    for i in range(1, 16):
        total = total + got5[i]
    got6[z] = total
    for i in range(1, 4):
        put(got6.at[z], got6.at[z], send.at[7], recv.at[6], in_z(i)).start()
    drain(got6.at[pl.ds(0, 3)], recv.at[6])
    got7[y] = (got6[0] + got6[1]) + (got6[2] + got6[3])
    for i in range(1, 8):
        put(got7.at[y], got7.at[y], send.at[8], recv.at[7], in_y(i)).start()
    drain(got7.at[pl.ds(0, 7)], recv.at[7])
    total = got7[0]
    for i in range(1, 8):
        total = total + got7[i]
    here = kl_v.at[pl.ds(pl.multiple_of(8 * g, 8), 8), :]
    here[...] = total * (1.0 / 128)

    @pl.loop(1, 16)
    def _(i):
        other, device = in_group(i)
        put(here, here, send.at[9], recv.at[9], device).start()

    drain(kl_v.at[pl.ds(0, 120)], recv.at[9])
    kl_ref[...] = kl_v[...]

    drain(spec.at[pl.ds(0, 3)], send.at[0])
    drain(basis_in, send.at[1])
    drain(beam_in, send.at[2])
    drain(made.at[pl.ds(0, 7)], send.at[3])
    drain(got.at[pl.ds(0, 15)], send.at[4])
    drain(rows.at[pl.ds(0, 120)], send.at[5])
    drain(got5.at[pl.ds(0, 15)], send.at[6])
    drain(got6.at[pl.ds(0, 3)], send.at[7])
    drain(got7.at[pl.ds(0, 7)], send.at[8])
    drain(kl_v.at[pl.ds(0, 120)], send.at[9])


def per_device(beams, basis, foreground, signal, band_start, band_width):
    anywhere = pl.BlockSpec(memory_space=pl.ANY)
    scalars = pl.BlockSpec(memory_space=pltpu.SMEM)
    vector = pl.BlockSpec(memory_space=pltpu.VMEM)
    return pl.pallas_call(
        kernel,
        out_shape=(
            jax.ShapeDtypeStruct((64, 128), F32),
            jax.ShapeDtypeStruct((128, 128), F32),
        ),
        in_specs=[anywhere] * 4 + [scalars] * 2,
        out_specs=(vector, vector),
        scratch_shapes=[
            pltpu.VMEM((256, 256), BF16),
            pltpu.VMEM((256, 128), BF16),
            pltpu.VMEM((64, 128), BF16),
            pltpu.VMEM((8, 4, 256), F32),
            pltpu.VMEM((8, 4, 256), F32),
            pltpu.VMEM((128, 256), BF16),
            pltpu.VMEM((32, 256), BF16),
            pltpu.VMEM((8, 32, 256), BF16),
            pltpu.VMEM((64, 256), BF16),
            pltpu.VMEM((4, 32, 256), F32),
            pltpu.VMEM((16, 32, 256), BF16),
            pltpu.VMEM((16, 32, 256), BF16),
            pltpu.VMEM((32, 256), F32),
            pltpu.VMEM((128, 256), F32),
            pltpu.VMEM((128, 128), F32),
            pltpu.VMEM((16, 8, 128), F32),
            pltpu.VMEM((4, 8, 128), F32),
            pltpu.VMEM((8, 8, 128), F32),
            pltpu.VMEM((128, 128), F32),
            pltpu.SemaphoreType.DMA((5,)),
            pltpu.SemaphoreType.DMA((10,)),
            pltpu.SemaphoreType.DMA((10,)),
        ],
        compiler_params=pltpu.CompilerParams(
            collective_id=0, has_side_effects=True, vmem_limit_bytes=60 << 20
        ),
    )(beams, basis, foreground, signal, band_start, band_width)


def solution(mesh):
    placed = (
        P("narrow", None, None),
        P("wide", None),
        P("narrow", "wide", None),
        P("narrow", "wide", None),
        P("narrow"),
        P("narrow"),
    )
    return jax.shard_map(
        per_device,
        mesh=mesh,
        in_specs=placed,
        out_specs=(P(("wide", "narrow"), None), P()),
        check_vma=False,
    )
```

time: 88 us -> 64.3 us (0.73)
  Pallas kernels: 80.7 us -> 61.4 us
  local copies, waits for them, and re-layouts: 6.24 us -> 2.04 us
    pallas_call x1, Pallas kernels: 80.7 us -> 61.4 us  [per_device(): pl.pallas_call(kernel, out_shape=(jax.ShapeDtypeStruct((64, 128), F32), j...]
    unnamed x14 -> x4, local copies, waits for them, and re-layouts: 6.24 us -> 2.04 us
where the time goes in v2:
time: 64.3 us; the launch traced here: 64.1 us
  Pallas kernels  61.4 us (95%)
  local copies, waits for them, and re-layouts  2.04 us (3%)
  between operations  0.65 us (1%)
    pallas_call x1, Pallas kernels, per_device(): pl.pallas_call(kernel, out_shape=(jax.ShapeDtypeStruct((64, 128), F32), j...  61.4 us
    unnamed x4, local copies, waits for them, and re-layouts  2.04 us

profile of v2, /device:TPU:1, one launch (start us, length us, event | category | flops | bytes accessed | tf_op | source)
XLA Modules:
  0.0 64.1 jit_solution(6289949647848951278)
XLA Ops:
  0.6 61.4 %shard_map.77 = (f32[64,128]{1,0:T(8,128)}, f32[128,128]{1,0:T(8,128)}) custom-call(bf16[8,256,256]{2,1,0:T(8,128)(2,1)} %beams_hbm.1, bf16[1024,128]{1,0:T(8,128)(2,1)} %basis_hbm.1, f32[8,4,256]{2,1,0:T(4,128)} %fore_hbm.1, f32[8,4,256]{2,1,0:T(4,128)} %sig_hbm.1, s32[8]{0:T(128)} %start_ref.1, s32[8]{0:T(128)} %width_ref.1), custom_call_target="tpu_custom_call" | custom-call | tf_op jit(solution)/shard_map/pallas_call | solution.py:228
  62.1 0.0 copy-start
  62.1 1.4 %copy.10 = f32[64,128]{1,0:T(8,128)} copy(f32[64,128]{1,0:T(8,128)} %get-tuple-element.4) | data formatting | bytes 65536
  63.5 0.0 copy-done
  63.5 0.6 copy.11
Async XLA Ops:
  62.1 1.4 %copy-start = (f32[128,128]{1,0:T(8,128)S(1)}, f32[128,128]{1,0:T(8,128)}, u32[]{:S(2)}) copy-start(f32[128,128]{1,0:T(8,128)} %get-tuple-element.5) | copy-start | bytes 196612

commit v3 on v2

v3 whole, which is shorter than its diff:
```python
import jax
import jax.numpy as jnp
from jax import lax
from jax.experimental import pallas as pl
from jax.experimental.pallas import tpu as pltpu
from jax.sharding import PartitionSpec as P

MESH = pl.DeviceIdType.MESH
F32 = jnp.float32
BF16 = jnp.bfloat16
NT = (((1,), (1,)), ((), ()))


def nt(a, b):
    return lax.dot_general(a, b, NT, preferred_element_type=F32)


def split(value):
    high = value.astype(BF16)
    return high, (value - high.astype(F32)).astype(BF16)


def put(src, dst, send, recv, device):
    return pltpu.make_async_remote_copy(
        src_ref=src, dst_ref=dst, send_sem=send, recv_sem=recv, device_id=device, device_id_type=MESH
    )


def drain(ref, sem):
    pltpu.make_async_copy(ref, ref, sem).wait()


def kernel(
    beams_hbm, basis_hbm, fore_hbm, sig_hbm, start_ref, width_ref, proj_ref, kl_ref,
    beam_v, block_v, fore_v, sig_v, basis_t, basis_in, made, beam_f, basis_f, spec, part, got, half, halves, square,
    term, got5, got6, got7, kl_v, local, send, recv,
):
    w = lax.axis_index("wide")
    n = lax.axis_index("narrow")
    y, q = lax.div(w, 4), lax.rem(w, 4)
    z, x = lax.div(n, 4), lax.rem(n, 4)
    chip, core = lax.div(w, 2), lax.rem(w, 2)
    g = x * 4 + q

    offset = lax.rem(x - lax.rem(chip, 4) + 4, 4)
    gives_basis = (lax.div(chip, 4) == z) & (lax.rem(offset, 2) == 1)
    first = lax.div(offset, 2)
    basis_source = (2 * n + lax.div(y, 4), 4 * z + lax.rem(x + 1 + 2 * lax.rem(y, 2), 4))
    gives_beams = lax.div(n, 2) == y
    own_beam = (x == 0) | (x == 3)

    load_fore = pltpu.make_async_copy(fore_hbm, fore_v, local.at[1])
    load_sig = pltpu.make_async_copy(sig_hbm, sig_v, local.at[2])
    load_beam = pltpu.make_async_copy(beams_hbm.at[y], beam_v, local.at[3])

    def load_block(i):
        row = pl.multiple_of(256 * (first + 2 * i), 256)
        return pltpu.make_async_copy(basis_hbm.at[pl.ds(row, 256), :], block_v.at[i], local.at[4 + i])

    @pl.when(gives_basis)
    def _():
        load_block(0).start()
        load_block(1).start()

    load_fore.start()
    load_sig.start()
    load_beam.start()

    def in_narrow(i):
        other = lax.rem(n + i, 16)
        return other, (w, other)

    def in_group(i):
        other = lax.rem(g + i, 16)
        return other, (y * 4 + lax.rem(other, 4), z * 4 + lax.div(other, 4))

    def in_y(i):
        return (4 * lax.rem(y + i, 8) + q, n)

    def in_q(i):
        return (4 * y + lax.rem(q + i, 4), n)

    barrier = pltpu.get_barrier_semaphore()

    def greet(device):
        pl.semaphore_signal(barrier, inc=1, device_id=device, device_id_type=MESH)

    greet(basis_source)

    @pl.loop(1, 16)
    def _(i):
        greet(in_narrow(i)[1])
        greet(in_group(i)[1])

    @pl.loop(1, 8)
    def _(i):
        greet(in_y(i))

    @pl.when(gives_basis)
    def _():
        for i in range(2):
            load_block(i).wait()
            basis_t[i] = block_v[i].astype(F32).T.astype(BF16)

    load_fore.wait()
    load_sig.wait()
    column = 4 * w + lax.broadcasted_iota(jnp.int32, (4, 256), 0)
    for f in range(8):
        low = start_ref[f]
        inband = ((column >= low) & (column < low + width_ref[f])).astype(F32)
        spec[q, pl.ds(4 * f, 4), :] = fore_v[f] + inband * sig_v[f]

    pl.semaphore_wait(barrier, 37 + 8 * gives_basis.astype(jnp.int32))

    @pl.when(gives_basis)
    def _():
        for i in range(2):
            for r in range(4):
                device = (4 * (4 * core + first + 2 * i) + r, chip)
                put(basis_t.at[i, pl.ds(32 * r, 32), :], basis_in, send.at[1], recv.at[1], device).start()

    for i in range(1, 4):
        put(spec.at[q], spec.at[q], send.at[0], recv.at[0], in_q(i)).start()
    quarter = beam_f.at[pl.ds(pl.multiple_of(64 * q, 64), 64), :]

    @pl.when(gives_beams)
    def _():
        for i in range(8):
            other = 4 * (i // 2) + 2 * lax.rem(n, 2) + i % 2
            source = beams_hbm.at[4 * (i % 2) + i // 2, pl.ds(pl.multiple_of(64 * q, 64), 64), :]

            @pl.when(other == n)
            def _():
                pltpu.make_async_copy(source, quarter, recv.at[2]).start()

            @pl.when(other != n)
            def _():
                put(source, quarter, send.at[2], recv.at[2], (w, other)).start()

    @pl.when(q == x)
    def _():
        source = basis_hbm.at[pl.ds(pl.multiple_of(256 * z, 256), 256), :]
        pltpu.make_async_copy(source, basis_f, recv.at[3]).start()
        for i in range(1, 4):
            put(source, basis_f, send.at[3], recv.at[3], in_q(i)).start()

    load_beam.wait()
    drain(basis_in, recv.at[1])
    made[y] = jnp.dot(basis_in[...], beam_v[...], preferred_element_type=F32).astype(BF16)

    for i in range(1, 8):
        put(made.at[y], made.at[y], send.at[4], recv.at[4], in_y(i)).start()
    drain(quarter, recv.at[2])
    for i in range(1, 4):
        put(quarter, quarter, send.at[5], recv.at[5], in_q(i)).start()
    drain(spec.at[pl.ds(0, 3)], recv.at[0])
    drain(made.at[pl.ds(0, 7)], recv.at[4])

    wide_made = [made[f].astype(F32) for f in range(8)]
    for step in range(4):
        to_z = lax.rem(z + 1 + step, 4)
        for r in range(4):
            total = spec[r, pl.ds(to_z, 1), :] * wide_made[0]
            for f in range(1, 8):
                total = total + spec[r, pl.ds(4 * f + to_z, 1), :] * wide_made[f]
            part[4 * to_z + r] = total.astype(BF16)
        for r in range(4):
            other = 4 * to_z + r

            @pl.when(other != n)
            def _():
                put(part.at[other], got.at[n], send.at[6], recv.at[6], (w, other)).start()

    got[n] = part[n]
    drain(beam_f.at[pl.ds(0, 192), :], recv.at[5])
    drain(basis_f, recv.at[3])
    drain(got.at[pl.ds(0, 15)], recv.at[6])
    total = got[0].astype(F32)
    for i in range(1, 16):
        total = total + got[i].astype(F32)

    high, low = split(total)
    turned = nt(high, beam_f[...]) + nt(low, beam_f[...])
    turned_high, turned_low = split(turned)
    term[...] = jnp.dot(turned_high, basis_f[...], preferred_element_type=F32) + jnp.dot(
        turned_low, basis_f[...], preferred_element_type=F32
    )

    for i in range(1, 4):
        to_x = lax.rem(x + i, 4)
        source = term.at[pl.ds(pl.multiple_of(8 * to_x, 8), 8), :]
        put(source, got5.at[x], send.at[8], recv.at[8], (w, 4 * z + to_x)).start()
    half[0] = turned[:, 0:128]
    half[1] = turned[:, 128:256]
    for to_x in range(4):
        same = (q == x) & (x == to_x)

        @pl.when(same)
        def _():
            pltpu.make_async_copy(half.at[to_x // 2], halves.at[q], recv.at[7]).start()

        @pl.when(jnp.logical_not(same))
        def _():
            put(half.at[to_x // 2], halves.at[q], send.at[7], recv.at[7], (4 * y + x, 4 * z + to_x)).start()

    got5[x] = term[pl.ds(pl.multiple_of(8 * x, 8), 8), :]
    drain(got5.at[pl.ds(0, 3)], recv.at[8])
    got6[z] = (got5[0] + got5[1]) + (got5[2] + got5[3])

    for i in range(1, 4):
        put(got6.at[z], got6.at[z], send.at[9], recv.at[9], (w, 4 * lax.rem(z + i, 4) + x)).start()
    drain(halves, recv.at[7])
    square[...] = halves[...].reshape(128, 128).T
    proj_ref[...] = square[pl.ds(pl.multiple_of(64 * lax.rem(x, 2), 64), 64), :]
    drain(got6.at[pl.ds(0, 3)], recv.at[9])
    got7[y] = (got6[0] + got6[1]) + (got6[2] + got6[3])
    for i in range(1, 8):
        put(got7.at[y], got7.at[y], send.at[10], recv.at[10], in_y(i)).start()
    drain(got7.at[pl.ds(0, 7)], recv.at[10])
    total = got7[0]
    for i in range(1, 8):
        total = total + got7[i]
    here = kl_v.at[pl.ds(pl.multiple_of(32 * q + 8 * x, 8), 8), :]
    here[...] = total * (1.0 / 128)

    @pl.loop(1, 16)
    def _(i):
        other, device = in_group(i)
        put(here, here, send.at[11], recv.at[11], device).start()

    drain(kl_v.at[pl.ds(0, 120)], recv.at[11])
    kl_ref[...] = kl_v[...]

    drain(spec.at[pl.ds(0, 3)], send.at[0])

    @pl.when(gives_basis)
    def _():
        drain(basis_t, send.at[1])

    @pl.when(gives_beams & own_beam)
    def _():
        drain(got.at[pl.ds(0, 14)], send.at[2])

    @pl.when(gives_beams & jnp.logical_not(own_beam))
    def _():
        drain(got, send.at[2])

    @pl.when(q == x)
    def _():
        drain(got.at[pl.ds(0, 12)], send.at[3])

    drain(made.at[pl.ds(0, 7)], send.at[4])
    drain(beam_f.at[pl.ds(0, 192), :], send.at[5])
    drain(got.at[pl.ds(0, 15)], send.at[6])

    @pl.when(q == x)
    def _():
        drain(halves.at[pl.ds(0, 3)], send.at[7])

    @pl.when(q != x)
    def _():
        drain(halves, send.at[7])

    drain(got5.at[pl.ds(0, 3)], send.at[8])
    drain(got6.at[pl.ds(0, 3)], send.at[9])
    drain(got7.at[pl.ds(0, 7)], send.at[10])
    drain(kl_v.at[pl.ds(0, 120)], send.at[11])


def per_device(beams, basis, foreground, signal, band_start, band_width):
    anywhere = pl.BlockSpec(memory_space=pl.ANY)
    scalars = pl.BlockSpec(memory_space=pltpu.SMEM)
    vector = pl.BlockSpec(memory_space=pltpu.VMEM)
    return pl.pallas_call(
        kernel,
        out_shape=(
            jax.ShapeDtypeStruct((64, 128), F32),
            jax.ShapeDtypeStruct((128, 128), F32),
        ),
        in_specs=[anywhere] * 4 + [scalars] * 2,
        out_specs=(vector, vector),
        scratch_shapes=[
            pltpu.VMEM((256, 256), BF16),
            pltpu.VMEM((2, 256, 128), BF16),
            pltpu.VMEM((8, 4, 256), F32),
            pltpu.VMEM((8, 4, 256), F32),
            pltpu.VMEM((2, 128, 256), BF16),
            pltpu.VMEM((32, 256), BF16),
            pltpu.VMEM((8, 32, 256), BF16),
            pltpu.VMEM((256, 256), BF16),
            pltpu.VMEM((256, 128), BF16),
            pltpu.VMEM((4, 32, 256), F32),
            pltpu.VMEM((16, 32, 256), BF16),
            pltpu.VMEM((16, 32, 256), BF16),
            pltpu.VMEM((2, 32, 128), F32),
            pltpu.VMEM((4, 32, 128), F32),
            pltpu.VMEM((128, 128), F32),
            pltpu.VMEM((32, 128), F32),
            pltpu.VMEM((4, 8, 128), F32),
            pltpu.VMEM((4, 8, 128), F32),
            pltpu.VMEM((8, 8, 128), F32),
            pltpu.VMEM((128, 128), F32),
            pltpu.SemaphoreType.DMA((6,)),
            pltpu.SemaphoreType.DMA((12,)),
            pltpu.SemaphoreType.DMA((12,)),
        ],
        compiler_params=pltpu.CompilerParams(
            collective_id=0, has_side_effects=True, vmem_limit_bytes=60 << 20
        ),
    )(beams, basis, foreground, signal, band_start, band_width)


def solution(mesh):
    placed = (
        P("narrow", None, None),
        P("wide", None),
        P("narrow", "wide", None),
        P("narrow", "wide", None),
        P("narrow"),
        P("narrow"),
    )
    return jax.shard_map(
        per_device,
        mesh=mesh,
        in_specs=placed,
        out_specs=(P(("wide", "narrow"), None), P()),
        check_vma=False,
    )
```

time: 64.3 us -> 57.6 us (0.90)
  Pallas kernels: 61.4 us -> 54.8 us
    pallas_call x1, Pallas kernels: 61.4 us -> 54.8 us  [per_device(): pl.pallas_call(kernel, out_shape=(jax.ShapeDtypeStruct((64, 128), F32), j...]
where the time goes in v3:
time: 57.6 us; the launch traced here: 57.5 us
  Pallas kernels  54.8 us (95%)
  local copies, waits for them, and re-layouts  2.04 us (4%)
  between operations  0.65 us (1%)
    pallas_call x1, Pallas kernels, per_device(): pl.pallas_call(kernel, out_shape=(jax.ShapeDtypeStruct((64, 128), F32), j...  54.8 us
    unnamed x4, local copies, waits for them, and re-layouts  2.04 us

profile of v3, /device:TPU:1, one launch (start us, length us, event | category | flops | bytes accessed | tf_op | source)
XLA Modules:
  0.0 57.5 jit_solution(2883544749317202271)
XLA Ops:
  0.6 54.8 %shard_map.77 = (f32[64,128]{1,0:T(8,128)}, f32[128,128]{1,0:T(8,128)}) custom-call(bf16[8,256,256]{2,1,0:T(8,128)(2,1)} %beams_hbm.1, bf16[1024,128]{1,0:T(8,128)(2,1)} %basis_hbm.1, f32[8,4,256]{2,1,0:T(4,128)} %fore_hbm.1, f32[8,4,256]{2,1,0:T(4,128)} %sig_hbm.1, s32[8]{0:T(128)} %start_ref.1, s32[8]{0:T(128)} %width_ref.1), custom_call_target="tpu_custom_call" | custom-call | tf_op jit(solution)/shard_map/pallas_call | solution.py:274
  55.4 0.0 copy-start
  55.4 1.4 %copy.10 = f32[64,128]{1,0:T(8,128)} copy(f32[64,128]{1,0:T(8,128)} %get-tuple-element.4) | data formatting | bytes 65536
  56.8 0.0 copy-done
  56.8 0.6 %copy.11 = f32[128,128]{1,0:T(8,128)} copy(f32[128,128]{1,0:T(8,128)S(1)} %copy-done) | data formatting | bytes 131072
Async XLA Ops:
  55.4 1.4 %copy-start = (f32[128,128]{1,0:T(8,128)S(1)}, f32[128,128]{1,0:T(8,128)}, u32[]{:S(2)}) copy-start(f32[128,128]{1,0:T(8,128)} %get-tuple-element.5) | copy-start | bytes 196612

commit v4 on v3

--- a/solution.py
+++ b/solution.py
@@ -274,8 +274,8 @@
     return pl.pallas_call(
         kernel,
         out_shape=(
-            jax.ShapeDtypeStruct((64, 128), F32),
-            jax.ShapeDtypeStruct((128, 128), F32),
+            pltpu.VMEM((64, 128), F32),
+            pltpu.VMEM((128, 128), F32),
         ),
         in_specs=[anywhere] * 4 + [scalars] * 2,
         out_specs=(vector, vector),

time: 57.6 us -> 56.2 us (0.976)
  local copies, waits for them, and re-layouts: 2.04 us -> 1.25 us
  Pallas kernels: 54.8 us -> 54.2 us
    unnamed x4 -> x2, local copies, waits for them, and re-layouts: 2.04 us -> 1.25 us
    pallas_call x1, Pallas kernels: 54.8 us -> 54.2 us  [per_device(): pl.pallas_call(kernel, out_shape=(pltpu.VMEM((64, 128), F32), pltpu.VMEM(...]
where the time goes in v4:
time: 56.2 us; the launch traced here: 56 us
  Pallas kernels  54.2 us (96%)
  local copies, waits for them, and re-layouts  1.25 us (2%)
  between operations  0.64 us (1%)
    pallas_call x1, Pallas kernels, per_device(): pl.pallas_call(kernel, out_shape=(pltpu.VMEM((64, 128), F32), pltpu.VMEM(...  54.2 us
    unnamed x2, local copies, waits for them, and re-layouts  1.25 us

profile of v4, /device:TPU:1, one launch (start us, length us, event | category | flops | bytes accessed | tf_op | source)
XLA Modules:
  0.0 56.0 jit_solution(13209495871764118205)
XLA Ops:
  0.6 54.2 %shard_map.77 = (f32[64,128]{1,0:T(8,128)S(1)}, f32[128,128]{1,0:T(8,128)S(1)}) custom-call(bf16[8,256,256]{2,1,0:T(8,128)(2,1)} %beams_hbm.1, bf16[1024,128]{1,0:T(8,128)(2,1)} %basis_hbm.1, f32[8,4,256]{2,1,0:T(4,128)} %fore_hbm.1, f32[8,4,256]{2,1,0:T(4,128)} %sig_hbm.1, s32[8]{0:T(128)} %start_ref.1, s32[8]{0:T(128)} %width_ref.1), custom_call_target="tpu_custom_call" | custom-call | tf_op jit(solution)/shard_map/pallas_call | solution.py:274
  54.8 0.6 %copy.10 = f32[64,128]{1,0:T(8,128)} copy(f32[64,128]{1,0:T(8,128)S(1)} %get-tuple-element.2) | data formatting | bytes 65536
  55.4 0.6 %copy.11 = f32[128,128]{1,0:T(8,128)} copy(f32[128,128]{1,0:T(8,128)S(1)} %get-tuple-element.3) | data formatting | bytes 131072

commit v5 on v4

v5 whole, which is shorter than its diff:
```python
import jax
import jax.numpy as jnp
from jax import lax
from jax.experimental import pallas as pl
from jax.experimental.pallas import tpu as pltpu
from jax.sharding import PartitionSpec as P

MESH = pl.DeviceIdType.MESH
F32 = jnp.float32
BF16 = jnp.bfloat16
NT = (((1,), (1,)), ((), ()))


def nt(a, b):
    return lax.dot_general(a, b, NT, preferred_element_type=F32)


def split(value):
    high = value.astype(BF16)
    return high, (value - high.astype(F32)).astype(BF16)


def put(src, dst, send, recv, device):
    return pltpu.make_async_remote_copy(
        src_ref=src, dst_ref=dst, send_sem=send, recv_sem=recv, device_id=device, device_id_type=MESH
    )


def drain(ref, sem):
    pltpu.make_async_copy(ref, ref, sem).wait()


def kernel(
    beams_hbm, basis_hbm, fore_hbm, sig_hbm, start_ref, width_ref, proj_ref, kl_ref,
    beam_v, block_v, fore_v, sig_v, basis_t, basis_in, made, pieces, wide, beam_f, basis_f, flipped, beam_in, prod, spec, part,
    got, mine, rows, got6, got7, kl_v, local, send, recv,
):
    w = lax.axis_index("wide")
    n = lax.axis_index("narrow")
    y, q = lax.div(w, 4), lax.rem(w, 4)
    z, x = lax.div(n, 4), lax.rem(n, 4)
    chip, core = lax.div(w, 2), lax.rem(w, 2)
    g = x * 4 + q

    offset = lax.rem(x - lax.rem(chip, 4) + 4, 4)
    gives_basis = (lax.div(chip, 4) == z) & (lax.rem(offset, 2) == 1)
    first = lax.div(offset, 2)
    basis_source = (2 * n + lax.div(y, 4), 4 * z + lax.rem(x + 1 + 2 * lax.rem(y, 2), 4))
    gives_beams = lax.div(n, 2) == y
    own_beam = (x == 0) | (x == 3)
    beam_source = 2 * y + lax.div(x, 2)

    load_fore = pltpu.make_async_copy(fore_hbm, fore_v, local.at[1])
    load_sig = pltpu.make_async_copy(sig_hbm, sig_v, local.at[2])
    load_beam = pltpu.make_async_copy(beams_hbm.at[y], beam_v, local.at[3])

    def load_block(i):
        row = pl.multiple_of(256 * (first + 2 * i), 256)
        return pltpu.make_async_copy(basis_hbm.at[pl.ds(row, 256), :], block_v.at[i], local.at[4 + i])

    @pl.when(gives_basis)
    def _():
        load_block(0).start()
        load_block(1).start()

    load_fore.start()
    load_sig.start()
    load_beam.start()

    def in_plane(i):
        other = lax.rem(4 * y + x + i, 32)
        return lax.rem(other, 4), (4 * lax.div(other, 4) + q, 4 * z + lax.rem(other, 4))

    def in_group(i):
        other = lax.rem(g + i, 16)
        return other, (y * 4 + lax.rem(other, 4), z * 4 + lax.div(other, 4))

    def in_y(i):
        return (4 * lax.rem(y + i, 8) + q, n)

    def in_z(i):
        return (w, 4 * lax.rem(z + i, 4) + x)

    def in_q(i):
        return (4 * y + lax.rem(q + i, 4), n)

    barrier = pltpu.get_barrier_semaphore()

    def greet(device):
        pl.semaphore_signal(barrier, inc=1, device_id=device, device_id_type=MESH)

    greet(basis_source)

    @pl.when(beam_source != n)
    def _():
        greet((w, beam_source))

    @pl.loop(1, 16)
    def _(i):
        greet(in_group(i)[1])

    @pl.loop(1, 32)
    def _(i):
        greet(in_plane(i)[1])

    for i in range(1, 4):
        greet(in_z(i))

    @pl.when(gives_basis)
    def _():
        for i in range(2):
            load_block(i).wait()
            basis_t[i] = block_v[i].astype(F32).T.astype(BF16)

    load_fore.wait()
    load_sig.wait()
    column = 4 * w + lax.broadcasted_iota(jnp.int32, (4, 256), 0)
    for f in range(8):
        low = start_ref[f]
        inband = ((column >= low) & (column < low + width_ref[f])).astype(F32)
        spec[g, pl.ds(4 * f, 4), :] = fore_v[f] + inband * sig_v[f]

    expected = 8 * gives_basis.astype(jnp.int32) + gives_beams.astype(jnp.int32) * (8 - own_beam.astype(jnp.int32))
    pl.semaphore_wait(barrier, 49 + expected)

    @pl.when(gives_basis)
    def _():
        for i in range(2):
            for r in range(4):
                device = (4 * (4 * core + first + 2 * i) + r, chip)
                put(basis_t.at[i, pl.ds(32 * r, 32), :], basis_in, send.at[1], recv.at[1], device).start()

    @pl.loop(1, 16)
    def _(i):
        put(spec.at[g], spec.at[g], send.at[0], recv.at[0], in_group(i)[1]).start()

    quarter = beam_f.at[pl.ds(pl.multiple_of(64 * q, 64), 64), :]

    @pl.when(gives_beams)
    def _():
        for i in range(8):
            other = 4 * (i // 2) + 2 * lax.rem(n, 2) + i % 2
            source = beams_hbm.at[4 * (i % 2) + i // 2, pl.ds(pl.multiple_of(64 * q, 64), 64), :]

            @pl.when(other == n)
            def _():
                pltpu.make_async_copy(source, quarter, recv.at[2]).start()

            @pl.when(other != n)
            def _():
                put(source, quarter, send.at[12], recv.at[2], (w, other)).start()

    @pl.when(q == x)
    def _():
        source = basis_hbm.at[pl.ds(pl.multiple_of(256 * z, 256), 256), :]
        pltpu.make_async_copy(source, basis_f, recv.at[3]).start()
        for i in range(1, 4):
            put(source, basis_f, send.at[3], recv.at[3], in_q(i)).start()

    load_beam.wait()
    drain(basis_in, recv.at[1])
    product = jnp.dot(basis_in[...], beam_v[...], preferred_element_type=F32)
    for r in range(4):
        made[r] = product[8 * r : 8 * r + 8].astype(BF16)

    me = 8 * x + y

    @pl.loop(1, 32)
    def _(i):
        to_x, device = in_plane(i)
        put(made.at[to_x], pieces.at[me], send.at[4], recv.at[4], device).start()

    pieces[me] = made[x]

    drain(quarter, recv.at[2])
    for i in range(1, 4):
        put(quarter, quarter, send.at[5], recv.at[5], in_q(i)).start()

    @pl.when(q == x)
    def _():
        pltpu.make_async_copy(quarter, beam_in, recv.at[7]).start()

    @pl.when(q != x)
    def _():
        put(quarter, beam_in, send.at[7], recv.at[7], (4 * y + x, 4 * z + q)).start()

    drain(basis_f, recv.at[3])
    lanes = pl.ds(pl.multiple_of(32 * q, 32), 32)
    drain(beam_f.at[pl.ds(0, 192), :], recv.at[5])
    flipped[...] = basis_f[...].astype(F32).T
    prod[g] = jnp.dot(flipped[lanes, :].astype(BF16), beam_f[...], preferred_element_type=F32).astype(BF16)

    drain(spec.at[pl.ds(0, 15)], recv.at[0])
    drain(pieces.at[pl.ds(0, 31)], recv.at[4])

    for i in range(32):
        wide[i] = pieces[i].astype(F32)
    for step in (2, 1, 3, 0):
        to_z = lax.rem(z + step, 4)
        for r in range(4):
            total = None
            for xx in range(4):
                for f in range(8):
                    item = spec[4 * xx + r, pl.ds(4 * f + to_z, 1), :] * wide[8 * xx + f]
                    total = item if total is None else total + item
            part[to_z, r] = total.astype(BF16)
        if step:
            put(part.at[to_z], got.at[z], send.at[6], recv.at[6], (w, 4 * to_z + x)).start()

    @pl.loop(1, 16)
    def _(i):
        put(prod.at[g], prod.at[g], send.at[2], recv.at[11], in_group(i)[1]).start()

    got[z] = part[z]
    drain(got.at[pl.ds(0, 3)], recv.at[6])
    drain(prod.at[pl.ds(0, 15)], recv.at[11])

    term = None
    for r in range(4):
        total = (got[0, r].astype(F32) + got[1, r].astype(F32)) + (got[2, r].astype(F32) + got[3, r].astype(F32))
        mine[r] = total
        high, low = split(total)
        for part_of in (high, low):
            item = jnp.concatenate([nt(part_of, prod[4 * r + c]) for c in range(4)], axis=1)
            term = item if term is None else term + item
    got6[z] = term

    for i in range(1, 4):
        put(got6.at[z], got6.at[z], send.at[9], recv.at[9], in_z(i)).start()

    place = pl.multiple_of(32 * q + 8 * x, 8)

    @pl.loop(1, 16)
    def _(i):
        other, device = in_group(i)
        put(mine.at[lax.rem(other, 4)], rows.at[pl.ds(place, 8), :], send.at[8], recv.at[8], device).start()

    rows[pl.ds(place, 8), :] = mine[q]
    drain(got6.at[pl.ds(0, 3)], recv.at[9])
    got7[y] = (got6[0] + got6[1]) + (got6[2] + got6[3])
    for i in range(1, 8):
        put(got7.at[y], got7.at[y], send.at[10], recv.at[10], in_y(i)).start()
    drain(beam_in, recv.at[7])
    drain(rows.at[pl.ds(0, 120)], recv.at[8])
    high, low = split(rows[...])
    chunk = beam_in[...]
    proj_ref[...] = nt(chunk, high) + nt(chunk, low)
    drain(got7.at[pl.ds(0, 7)], recv.at[10])
    total = got7[0]
    for i in range(1, 8):
        total = total + got7[i]
    here = kl_v.at[pl.ds(place, 8), :]
    here[...] = total * (1.0 / 128)

    @pl.loop(1, 16)
    def _(i):
        put(here, here, send.at[11], recv.at[12], in_group(i)[1]).start()

    drain(kl_v.at[pl.ds(0, 120)], recv.at[12])
    kl_ref[...] = kl_v[...]

    drain(spec.at[pl.ds(0, 15)], send.at[0])

    @pl.when(gives_basis)
    def _():
        drain(basis_t, send.at[1])

    @pl.when(gives_beams & own_beam)
    def _():
        drain(prod.at[pl.ds(0, 14)], send.at[12])

    @pl.when(gives_beams & jnp.logical_not(own_beam))
    def _():
        drain(prod, send.at[12])

    @pl.when(q == x)
    def _():
        drain(prod.at[pl.ds(0, 12)], send.at[3])

    @pl.when(q != x)
    def _():
        drain(beam_in, send.at[7])

    drain(prod.at[pl.ds(0, 15)], send.at[2])
    drain(pieces.at[pl.ds(0, 31)], send.at[4])
    drain(beam_f.at[pl.ds(0, 192), :], send.at[5])
    drain(got.at[pl.ds(0, 3)], send.at[6])
    drain(rows.at[pl.ds(0, 120)], send.at[8])
    drain(got6.at[pl.ds(0, 3)], send.at[9])
    drain(got7.at[pl.ds(0, 7)], send.at[10])
    drain(kl_v.at[pl.ds(0, 120)], send.at[11])


def per_device(beams, basis, foreground, signal, band_start, band_width):
    anywhere = pl.BlockSpec(memory_space=pl.ANY)
    scalars = pl.BlockSpec(memory_space=pltpu.SMEM)
    vector = pl.BlockSpec(memory_space=pltpu.VMEM)
    return pl.pallas_call(
        kernel,
        out_shape=(
            pltpu.VMEM((64, 128), F32),
            pltpu.VMEM((128, 128), F32),
        ),
        in_specs=[anywhere] * 4 + [scalars] * 2,
        out_specs=(vector, vector),
        scratch_shapes=[
            pltpu.VMEM((256, 256), BF16),
            pltpu.VMEM((2, 256, 128), BF16),
            pltpu.VMEM((8, 4, 256), F32),
            pltpu.VMEM((8, 4, 256), F32),
            pltpu.VMEM((2, 128, 256), BF16),
            pltpu.VMEM((32, 256), BF16),
            pltpu.VMEM((4, 8, 256), BF16),
            pltpu.VMEM((32, 8, 256), BF16),
            pltpu.VMEM((32, 8, 256), F32),
            pltpu.VMEM((256, 256), BF16),
            pltpu.VMEM((256, 128), BF16),
            pltpu.VMEM((128, 256), F32),
            pltpu.VMEM((64, 256), BF16),
            pltpu.VMEM((16, 32, 256), BF16),
            pltpu.VMEM((16, 32, 256), F32),
            pltpu.VMEM((4, 4, 8, 256), BF16),
            pltpu.VMEM((4, 4, 8, 256), BF16),
            pltpu.VMEM((4, 8, 256), F32),
            pltpu.VMEM((128, 256), F32),
            pltpu.VMEM((4, 8, 128), F32),
            pltpu.VMEM((8, 8, 128), F32),
            pltpu.VMEM((128, 128), F32),
            pltpu.SemaphoreType.DMA((6,)),
            pltpu.SemaphoreType.DMA((13,)),
            pltpu.SemaphoreType.DMA((13,)),
        ],
        compiler_params=pltpu.CompilerParams(
            collective_id=0, has_side_effects=True, vmem_limit_bytes=60 << 20
        ),
    )(beams, basis, foreground, signal, band_start, band_width)


def solution(mesh):
    placed = (
        P("narrow", None, None),
        P("wide", None),
        P("narrow", "wide", None),
        P("narrow", "wide", None),
        P("narrow"),
        P("narrow"),
    )
    return jax.shard_map(
        per_device,
        mesh=mesh,
        in_specs=placed,
        out_specs=(P(("wide", "narrow"), None), P()),
        check_vma=False,
    )
```

time: 56.2 us -> 54.5 us (0.970)
  Pallas kernels: 54.2 us -> 52.5 us
    pallas_call x1, Pallas kernels: 54.2 us -> 52.5 us  [per_device(): pl.pallas_call(kernel, out_shape=(pltpu.VMEM((64, 128), F32), pltpu.VMEM(...]
where the time goes in v5:
time: 54.5 us; the launch traced here: 54.3 us
  Pallas kernels  52.5 us (96%)
  local copies, waits for them, and re-layouts  1.25 us (2%)
  between operations  0.64 us (1%)
    pallas_call x1, Pallas kernels, per_device(): pl.pallas_call(kernel, out_shape=(pltpu.VMEM((64, 128), F32), pltpu.VMEM(...  52.5 us
    unnamed x2, local copies, waits for them, and re-layouts  1.25 us

profile of v5, /device:TPU:1, one launch (start us, length us, event | category | flops | bytes accessed | tf_op | source)
XLA Modules:
  0.0 54.3 jit_solution(17584076320469746677)
XLA Ops:
  0.6 52.5 %shard_map.77 = (f32[64,128]{1,0:T(8,128)S(1)}, f32[128,128]{1,0:T(8,128)S(1)}) custom-call(bf16[8,256,256]{2,1,0:T(8,128)(2,1)} %beams_hbm.1, bf16[1024,128]{1,0:T(8,128)(2,1)} %basis_hbm.1, f32[8,4,256]{2,1,0:T(4,128)} %fore_hbm.1, f32[8,4,256]{2,1,0:T(4,128)} %sig_hbm.1, s32[8]{0:T(128)} %start_ref.1, s32[8]{0:T(128)} %width_ref.1), custom_call_target="tpu_custom_call" | custom-call | tf_op jit(solution)/shard_map/pallas_call | solution.py:298
  53.1 0.6 %copy.10 = f32[64,128]{1,0:T(8,128)} copy(f32[64,128]{1,0:T(8,128)S(1)} %get-tuple-element.2) | data formatting | bytes 65536
  53.7 0.6 %copy.11 = f32[128,128]{1,0:T(8,128)} copy(f32[128,128]{1,0:T(8,128)S(1)} %get-tuple-element.3) | data formatting | bytes 131072

commit v6 on v5

--- a/solution.py
+++ b/solution.py
@@ -41,6 +41,9 @@
     z, x = lax.div(n, 4), lax.rem(n, 4)
     chip, core = lax.div(w, 2), lax.rem(w, 2)
     g = x * 4 + q
+    pair = 2 * x + lax.div(q, 2)
+    own = 8 * core + pair
+    sibling = (w + 1 - 2 * core, n)
 
     offset = lax.rem(x - lax.rem(chip, 4) + 4, 4)
     gives_basis = (lax.div(chip, 4) == z) & (lax.rem(offset, 2) == 1)
@@ -75,6 +78,10 @@
         other = lax.rem(g + i, 16)
         return other, (y * 4 + lax.rem(other, 4), z * 4 + lax.div(other, 4))
 
+    def in_core(i):
+        other = lax.rem(pair + i, 8)
+        return (4 * y + 2 * lax.rem(other, 2) + core, 4 * z + lax.div(other, 2))
+
     def in_y(i):
         return (4 * lax.rem(y + i, 8) + q, n)
 
@@ -118,7 +125,7 @@
     for f in range(8):
         low = start_ref[f]
         inband = ((column >= low) & (column < low + width_ref[f])).astype(F32)
-        spec[g, pl.ds(4 * f, 4), :] = fore_v[f] + inband * sig_v[f]
+        spec[own, pl.ds(4 * f, 4), :] = fore_v[f] + inband * sig_v[f]
 
     expected = 8 * gives_basis.astype(jnp.int32) + gives_beams.astype(jnp.int32) * (8 - own_beam.astype(jnp.int32))
     pl.semaphore_wait(barrier, 49 + expected)
@@ -130,9 +137,9 @@
                 device = (4 * (4 * core + first + 2 * i) + r, chip)
                 put(basis_t.at[i, pl.ds(32 * r, 32), :], basis_in, send.at[1], recv.at[1], device).start()
 
-    @pl.loop(1, 16)
-    def _(i):
-        put(spec.at[g], spec.at[g], send.at[0], recv.at[0], in_group(i)[1]).start()
+    @pl.loop(1, 8)
+    def _(i):
+        put(spec.at[own], spec.at[own], send.at[0], recv.at[0], in_core(i)).start()
 
     quarter = beam_f.at[pl.ds(pl.multiple_of(64 * q, 64), 64), :]
 
@@ -172,6 +179,10 @@
 
     pieces[me] = made[x]
 
+    drain(spec.at[pl.ds(0, 7)], recv.at[0])
+    ours = spec.at[pl.ds(pl.multiple_of(8 * core, 8), 8)]
+    put(ours, ours, send.at[13], recv.at[13], sibling).start()
+
     drain(quarter, recv.at[2])
     for i in range(1, 4):
         put(quarter, quarter, send.at[5], recv.at[5], in_q(i)).start()
@@ -184,13 +195,7 @@
     def _():
         put(quarter, beam_in, send.at[7], recv.at[7], (4 * y + x, 4 * z + q)).start()
 
-    drain(basis_f, recv.at[3])
-    lanes = pl.ds(pl.multiple_of(32 * q, 32), 32)
-    drain(beam_f.at[pl.ds(0, 192), :], recv.at[5])
-    flipped[...] = basis_f[...].astype(F32).T
-    prod[g] = jnp.dot(flipped[lanes, :].astype(BF16), beam_f[...], preferred_element_type=F32).astype(BF16)
-
-    drain(spec.at[pl.ds(0, 15)], recv.at[0])
+    drain(spec.at[pl.ds(0, 8)], recv.at[13])
     drain(pieces.at[pl.ds(0, 31)], recv.at[4])
 
     for i in range(32):
@@ -201,19 +206,28 @@
             total = None
             for xx in range(4):
                 for f in range(8):
-                    item = spec[4 * xx + r, pl.ds(4 * f + to_z, 1), :] * wide[8 * xx + f]
+                    item = spec[8 * (r % 2) + 2 * xx + r // 2, pl.ds(4 * f + to_z, 1), :] * wide[8 * xx + f]
                     total = item if total is None else total + item
             part[to_z, r] = total.astype(BF16)
         if step:
             put(part.at[to_z], got.at[z], send.at[6], recv.at[6], (w, 4 * to_z + x)).start()
 
-    @pl.loop(1, 16)
-    def _(i):
-        put(prod.at[g], prod.at[g], send.at[2], recv.at[11], in_group(i)[1]).start()
+    drain(basis_f, recv.at[3])
+    lanes = pl.ds(pl.multiple_of(32 * q, 32), 32)
+    drain(beam_f.at[pl.ds(0, 192), :], recv.at[5])
+    flipped[...] = basis_f[...].astype(F32).T
+    prod[own] = jnp.dot(flipped[lanes, :].astype(BF16), beam_f[...], preferred_element_type=F32).astype(BF16)
+
+    @pl.loop(1, 8)
+    def _(i):
+        put(prod.at[own], prod.at[own], send.at[2], recv.at[11], in_core(i)).start()
 
     got[z] = part[z]
+    drain(prod.at[pl.ds(0, 7)], recv.at[11])
+    shared = prod.at[pl.ds(pl.multiple_of(8 * core, 8), 8)]
+    put(shared, shared, send.at[14], recv.at[14], sibling).start()
     drain(got.at[pl.ds(0, 3)], recv.at[6])
-    drain(prod.at[pl.ds(0, 15)], recv.at[11])
+    drain(prod.at[pl.ds(0, 8)], recv.at[14])
 
     term = None
     for r in range(4):
@@ -221,7 +235,7 @@
         mine[r] = total
         high, low = split(total)
         for part_of in (high, low):
-            item = jnp.concatenate([nt(part_of, prod[4 * r + c]) for c in range(4)], axis=1)
+            item = jnp.concatenate([nt(part_of, prod[8 * (c % 2) + 2 * r + c // 2]) for c in range(4)], axis=1)
             term = item if term is None else term + item
     got6[z] = term
 
@@ -259,7 +273,8 @@
     drain(kl_v.at[pl.ds(0, 120)], recv.at[12])
     kl_ref[...] = kl_v[...]
 
-    drain(spec.at[pl.ds(0, 15)], send.at[0])
+    drain(spec.at[pl.ds(0, 7)], send.at[0])
+    drain(spec.at[pl.ds(0, 8)], send.at[13])
 
     @pl.when(gives_basis)
     def _():
@@ -281,7 +296,8 @@
     def _():
         drain(beam_in, send.at[7])
 
-    drain(prod.at[pl.ds(0, 15)], send.at[2])
+    drain(prod.at[pl.ds(0, 7)], send.at[2])
+    drain(prod.at[pl.ds(0, 8)], send.at[14])
     drain(pieces.at[pl.ds(0, 31)], send.at[4])
     drain(beam_f.at[pl.ds(0, 192), :], send.at[5])
     drain(got.at[pl.ds(0, 3)], send.at[6])
@@ -327,8 +343,8 @@
             pltpu.VMEM((8, 8, 128), F32),
             pltpu.VMEM((128, 128), F32),
             pltpu.SemaphoreType.DMA((6,)),
-            pltpu.SemaphoreType.DMA((13,)),
-            pltpu.SemaphoreType.DMA((13,)),
+            pltpu.SemaphoreType.DMA((15,)),
+            pltpu.SemaphoreType.DMA((15,)),
         ],
         compiler_params=pltpu.CompilerParams(
             collective_id=0, has_side_effects=True, vmem_limit_bytes=60 << 20

time: 54.5 us -> 52.3 us (0.960)
  Pallas kernels: 52.5 us -> 50.2 us
    pallas_call x1, Pallas kernels: 52.5 us -> 50.2 us  [per_device(): pl.pallas_call(kernel, out_shape=(pltpu.VMEM((64, 128), F32), pltpu.VMEM(...]
where the time goes in v6:
time: 52.3 us; the launch traced here: 52.1 us
  Pallas kernels  50.2 us (96%)
  local copies, waits for them, and re-layouts  1.25 us (2%)
  between operations  0.64 us (1%)
    pallas_call x1, Pallas kernels, per_device(): pl.pallas_call(kernel, out_shape=(pltpu.VMEM((64, 128), F32), pltpu.VMEM(...  50.2 us
    unnamed x2, local copies, waits for them, and re-layouts  1.25 us

profile of v6, /device:TPU:1, one launch (start us, length us, event | category | flops | bytes accessed | tf_op | source)
XLA Modules:
  0.0 52.1 jit_solution(16129167251230169086)
XLA Ops:
  0.6 50.2 %shard_map.77 = (f32[64,128]{1,0:T(8,128)S(1)}, f32[128,128]{1,0:T(8,128)S(1)}) custom-call(bf16[8,256,256]{2,1,0:T(8,128)(2,1)} %beams_hbm.1, bf16[1024,128]{1,0:T(8,128)(2,1)} %basis_hbm.1, f32[8,4,256]{2,1,0:T(4,128)} %fore_hbm.1, f32[8,4,256]{2,1,0:T(4,128)} %sig_hbm.1, s32[8]{0:T(128)} %start_ref.1, s32[8]{0:T(128)} %width_ref.1), custom_call_target="tpu_custom_call" | custom-call | tf_op jit(solution)/shard_map/pallas_call | solution.py:314
  50.9 0.6 %copy.10 = f32[64,128]{1,0:T(8,128)} copy(f32[64,128]{1,0:T(8,128)S(1)} %get-tuple-element.2) | data formatting | bytes 65536
  51.5 0.6 %copy.11 = f32[128,128]{1,0:T(8,128)} copy(f32[128,128]{1,0:T(8,128)S(1)} %get-tuple-element.3) | data formatting | bytes 131072

commit v7 on v6

--- a/solution.py
+++ b/solution.py
@@ -45,10 +45,9 @@
     own = 8 * core + pair
     sibling = (w + 1 - 2 * core, n)
 
-    offset = lax.rem(x - lax.rem(chip, 4) + 4, 4)
-    gives_basis = (lax.div(chip, 4) == z) & (lax.rem(offset, 2) == 1)
-    first = lax.div(offset, 2)
-    basis_source = (2 * n + lax.div(y, 4), 4 * z + lax.rem(x + 1 + 2 * lax.rem(y, 2), 4))
+    gives_basis = chip == n
+    basis_source = 2 * n + lax.div(y, 4)
+    own_basis = basis_source == w
     gives_beams = lax.div(n, 2) == y
     own_beam = (x == 0) | (x == 3)
     beam_source = 2 * y + lax.div(x, 2)
@@ -58,64 +57,63 @@
     load_beam = pltpu.make_async_copy(beams_hbm.at[y], beam_v, local.at[3])
 
     def load_block(i):
-        row = pl.multiple_of(256 * (first + 2 * i), 256)
-        return pltpu.make_async_copy(basis_hbm.at[pl.ds(row, 256), :], block_v.at[i], local.at[4 + i])
+        return pltpu.make_async_copy(basis_hbm.at[pl.ds(256 * i, 256), :], block_v.at[i], local.at[4 + i])
 
     @pl.when(gives_basis)
     def _():
-        load_block(0).start()
-        load_block(1).start()
+        for i in range(4):
+            load_block(i).start()
 
     load_fore.start()
     load_sig.start()
     load_beam.start()
 
-    def in_plane(i):
-        other = lax.rem(4 * y + x + i, 32)
-        return lax.rem(other, 4), (4 * lax.div(other, 4) + q, 4 * z + lax.rem(other, 4))
-
-    def in_group(i):
-        other = lax.rem(g + i, 16)
-        return other, (y * 4 + lax.rem(other, 4), z * 4 + lax.div(other, 4))
-
-    def in_core(i):
-        other = lax.rem(pair + i, 8)
-        return (4 * y + 2 * lax.rem(other, 2) + core, 4 * z + lax.div(other, 2))
+    ys = [lax.rem(y + i, 8) for i in range(8)]
+    xs = [lax.rem(x + i, 4) for i in range(4)]
+    zs = [lax.rem(z + i, 4) for i in range(4)]
+    qs = [lax.rem(q + i, 4) for i in range(4)]
+    half_q = lax.div(q, 2)
+    y_rows = [4 * other + q for other in ys]
+    x_columns = [4 * z + other for other in xs]
+    q_rows = [4 * y + other for other in qs]
+    z_columns = [4 * other + x for other in zs]
+    plane = [(xs[b], (y_rows[a], x_columns[b])) for a in range(8) for b in range(4)][1:]
+    group = [(xs[b], qs[a], (q_rows[a], x_columns[b])) for b in range(4) for a in range(4)][1:]
+    in_core = [(4 * y + 2 * lax.rem(half_q + a, 2) + core, x_columns[b]) for b in range(4) for a in range(2)][1:]
 
     def in_y(i):
-        return (4 * lax.rem(y + i, 8) + q, n)
+        return (y_rows[i], n)
 
     def in_z(i):
-        return (w, 4 * lax.rem(z + i, 4) + x)
+        return (w, z_columns[i])
 
     def in_q(i):
-        return (4 * y + lax.rem(q + i, 4), n)
+        return (q_rows[i], n)
 
     barrier = pltpu.get_barrier_semaphore()
 
     def greet(device):
         pl.semaphore_signal(barrier, inc=1, device_id=device, device_id_type=MESH)
 
-    greet(basis_source)
+    @pl.when(jnp.logical_not(own_basis))
+    def _():
+        greet((basis_source, n))
 
     @pl.when(beam_source != n)
     def _():
         greet((w, beam_source))
 
-    @pl.loop(1, 16)
-    def _(i):
-        greet(in_group(i)[1])
-
-    @pl.loop(1, 32)
-    def _(i):
-        greet(in_plane(i)[1])
+    for item in group:
+        greet(item[-1])
+    for item in plane:
+        greet(item[-1])
 
     for i in range(1, 4):
         greet(in_z(i))
 
     @pl.when(gives_basis)
     def _():
-        for i in range(2):
+        for i in range(4):
             load_block(i).wait()
             basis_t[i] = block_v[i].astype(F32).T.astype(BF16)
 
@@ -127,19 +125,26 @@
         inband = ((column >= low) & (column < low + width_ref[f])).astype(F32)
         spec[own, pl.ds(4 * f, 4), :] = fore_v[f] + inband * sig_v[f]
 
-    expected = 8 * gives_basis.astype(jnp.int32) + gives_beams.astype(jnp.int32) * (8 - own_beam.astype(jnp.int32))
+    expected = 16 * gives_basis.astype(jnp.int32) - own_basis.astype(jnp.int32) + gives_beams.astype(jnp.int32) * (8 - own_beam.astype(jnp.int32))
     pl.semaphore_wait(barrier, 49 + expected)
 
     @pl.when(gives_basis)
     def _():
-        for i in range(2):
+        for i in range(4):
             for r in range(4):
-                device = (4 * (4 * core + first + 2 * i) + r, chip)
-                put(basis_t.at[i, pl.ds(32 * r, 32), :], basis_in, send.at[1], recv.at[1], device).start()
-
-    @pl.loop(1, 8)
-    def _(i):
-        put(spec.at[own], spec.at[own], send.at[0], recv.at[0], in_core(i)).start()
+                other = 16 * core + 4 * i + r
+                source = basis_t.at[i, pl.ds(32 * r, 32), :]
+
+                @pl.when(other == w)
+                def _():
+                    pltpu.make_async_copy(source, basis_in, recv.at[1]).start()
+
+                @pl.when(other != w)
+                def _():
+                    put(source, basis_in, send.at[1], recv.at[1], (other, n)).start()
+
+    for device in in_core:
+        put(spec.at[own], spec.at[own], send.at[0], recv.at[0], device).start()
 
     quarter = beam_f.at[pl.ds(pl.multiple_of(64 * q, 64), 64), :]
 
@@ -172,9 +177,7 @@
 
     me = 8 * x + y
 
-    @pl.loop(1, 32)
-    def _(i):
-        to_x, device = in_plane(i)
+    for to_x, device in plane:
         put(made.at[to_x], pieces.at[me], send.at[4], recv.at[4], device).start()
 
     pieces[me] = made[x]
@@ -201,7 +204,7 @@
     for i in range(32):
         wide[i] = pieces[i].astype(F32)
     for step in (2, 1, 3, 0):
-        to_z = lax.rem(z + step, 4)
+        to_z = zs[step]
         for r in range(4):
             total = None
             for xx in range(4):
@@ -218,9 +221,8 @@
     flipped[...] = basis_f[...].astype(F32).T
     prod[own] = jnp.dot(flipped[lanes, :].astype(BF16), beam_f[...], preferred_element_type=F32).astype(BF16)
 
-    @pl.loop(1, 8)
-    def _(i):
-        put(prod.at[own], prod.at[own], send.at[2], recv.at[11], in_core(i)).start()
+    for device in in_core:
+        put(prod.at[own], prod.at[own], send.at[2], recv.at[11], device).start()
 
     got[z] = part[z]
     drain(prod.at[pl.ds(0, 7)], recv.at[11])
@@ -244,10 +246,8 @@
 
     place = pl.multiple_of(32 * q + 8 * x, 8)
 
-    @pl.loop(1, 16)
-    def _(i):
-        other, device = in_group(i)
-        put(mine.at[lax.rem(other, 4)], rows.at[pl.ds(place, 8), :], send.at[8], recv.at[8], device).start()
+    for to_x, to_q, device in group:
+        put(mine.at[to_q], rows.at[pl.ds(place, 8), :], send.at[8], recv.at[8], device).start()
 
     rows[pl.ds(place, 8), :] = mine[q]
     drain(got6.at[pl.ds(0, 3)], recv.at[9])
@@ -266,9 +266,8 @@
     here = kl_v.at[pl.ds(place, 8), :]
     here[...] = total * (1.0 / 128)
 
-    @pl.loop(1, 16)
-    def _(i):
-        put(here, here, send.at[11], recv.at[12], in_group(i)[1]).start()
+    for item in group:
+        put(here, here, send.at[11], recv.at[12], item[-1]).start()
 
     drain(kl_v.at[pl.ds(0, 120)], recv.at[12])
     kl_ref[...] = kl_v[...]
@@ -276,9 +275,13 @@
     drain(spec.at[pl.ds(0, 7)], send.at[0])
     drain(spec.at[pl.ds(0, 8)], send.at[13])
 
-    @pl.when(gives_basis)
-    def _():
-        drain(basis_t, send.at[1])
+    @pl.when(own_basis)
+    def _():
+        drain(prod.at[pl.ds(0, 15)], send.at[1])
+
+    @pl.when(gives_basis & jnp.logical_not(own_basis))
+    def _():
+        drain(prod, send.at[1])
 
     @pl.when(gives_beams & own_beam)
     def _():
@@ -321,10 +324,10 @@
         out_specs=(vector, vector),
         scratch_shapes=[
             pltpu.VMEM((256, 256), BF16),
-            pltpu.VMEM((2, 256, 128), BF16),
+            pltpu.VMEM((4, 256, 128), BF16),
             pltpu.VMEM((8, 4, 256), F32),
             pltpu.VMEM((8, 4, 256), F32),
-            pltpu.VMEM((2, 128, 256), BF16),
+            pltpu.VMEM((4, 128, 256), BF16),
             pltpu.VMEM((32, 256), BF16),
             pltpu.VMEM((4, 8, 256), BF16),
             pltpu.VMEM((32, 8, 256), BF16),
@@ -342,7 +345,7 @@
             pltpu.VMEM((4, 8, 128), F32),
             pltpu.VMEM((8, 8, 128), F32),
             pltpu.VMEM((128, 128), F32),
-            pltpu.SemaphoreType.DMA((6,)),
+            pltpu.SemaphoreType.DMA((8,)),
             pltpu.SemaphoreType.DMA((15,)),
             pltpu.SemaphoreType.DMA((15,)),
         ],

time: 52.3 us -> 51.2 us (0.979)
  Pallas kernels: 50.2 us -> 49.2 us
    pallas_call x1, Pallas kernels: 50.2 us -> 49.2 us  [per_device(): pl.pallas_call(kernel, out_shape=(pltpu.VMEM((64, 128), F32), pltpu.VMEM(...]
where the time goes in v7:
time: 51.2 us; the launch traced here: 51 us
  Pallas kernels  49.2 us (96%)
  local copies, waits for them, and re-layouts  1.25 us (2%)
  between operations  0.64 us (1%)
    pallas_call x1, Pallas kernels, per_device(): pl.pallas_call(kernel, out_shape=(pltpu.VMEM((64, 128), F32), pltpu.VMEM(...  49.2 us
    unnamed x2, local copies, waits for them, and re-layouts  1.25 us

profile of v7, /device:TPU:1, one launch (start us, length us, event | category | flops | bytes accessed | tf_op | source)
XLA Modules:
  0.0 51.0 jit_solution(10522843185830739828)
XLA Ops:
  0.6 49.2 %shard_map.77 = (f32[64,128]{1,0:T(8,128)S(1)}, f32[128,128]{1,0:T(8,128)S(1)}) custom-call(bf16[8,256,256]{2,1,0:T(8,128)(2,1)} %beams_hbm.1, bf16[1024,128]{1,0:T(8,128)(2,1)} %basis_hbm.1, f32[8,4,256]{2,1,0:T(4,128)} %fore_hbm.1, f32[8,4,256]{2,1,0:T(4,128)} %sig_hbm.1, s32[8]{0:T(128)} %start_ref.1, s32[8]{0:T(128)} %width_ref.1), custom_call_target="tpu_custom_call" | custom-call | tf_op jit(solution)/shard_map/pallas_call | solution.py:317
  49.8 0.6 %copy.10 = f32[64,128]{1,0:T(8,128)} copy(f32[64,128]{1,0:T(8,128)S(1)} %get-tuple-element.2) | data formatting | bytes 65536
  50.4 0.6 %copy.11 = f32[128,128]{1,0:T(8,128)} copy(f32[128,128]{1,0:T(8,128)S(1)} %get-tuple-element.3) | data formatting | bytes 131072

commit v8 on v7

--- a/solution.py
+++ b/solution.py
@@ -246,14 +246,15 @@
 
     place = pl.multiple_of(32 * q + 8 * x, 8)
 
-    for to_x, to_q, device in group:
-        put(mine.at[to_q], rows.at[pl.ds(place, 8), :], send.at[8], recv.at[8], device).start()
-
     rows[pl.ds(place, 8), :] = mine[q]
     drain(got6.at[pl.ds(0, 3)], recv.at[9])
     got7[y] = (got6[0] + got6[1]) + (got6[2] + got6[3])
     for i in range(1, 8):
         put(got7.at[y], got7.at[y], send.at[10], recv.at[10], in_y(i)).start()
+
+    for to_x, to_q, device in group:
+        put(mine.at[to_q], rows.at[pl.ds(place, 8), :], send.at[8], recv.at[8], device).start()
+
     drain(beam_in, recv.at[7])
     drain(rows.at[pl.ds(0, 120)], recv.at[8])
     high, low = split(rows[...])

time: 51.2 us -> 51.1 us (level)
  no operation moved by 1% of the time
where the time goes in v8:
time: 51.1 us; the launch traced here: 51 us
  Pallas kernels  49.1 us (96%)
  local copies, waits for them, and re-layouts  1.25 us (2%)
  between operations  0.64 us (1%)
    pallas_call x1, Pallas kernels, per_device(): pl.pallas_call(kernel, out_shape=(pltpu.VMEM((64, 128), F32), pltpu.VMEM(...  49.1 us
    unnamed x2, local copies, waits for them, and re-layouts  1.25 us

profile of v8, /device:TPU:1, one launch (start us, length us, event | category | flops | bytes accessed | tf_op | source)
XLA Modules:
  0.0 51.0 jit_solution(4053859225391539192)
XLA Ops:
  0.6 49.1 %shard_map.77 = (f32[64,128]{1,0:T(8,128)S(1)}, f32[128,128]{1,0:T(8,128)S(1)}) custom-call(bf16[8,256,256]{2,1,0:T(8,128)(2,1)} %beams_hbm.1, bf16[1024,128]{1,0:T(8,128)(2,1)} %basis_hbm.1, f32[8,4,256]{2,1,0:T(4,128)} %fore_hbm.1, f32[8,4,256]{2,1,0:T(4,128)} %sig_hbm.1, s32[8]{0:T(128)} %start_ref.1, s32[8]{0:T(128)} %width_ref.1), custom_call_target="tpu_custom_call" | custom-call | tf_op jit(solution)/shard_map/pallas_call | solution.py:318
  49.7 0.6 %copy.10 = f32[64,128]{1,0:T(8,128)} copy(f32[64,128]{1,0:T(8,128)S(1)} %get-tuple-element.2) | data formatting | bytes 65536
  50.3 0.6 %copy.11 = f32[128,128]{1,0:T(8,128)} copy(f32[128,128]{1,0:T(8,128)S(1)} %get-tuple-element.3) | data formatting | bytes 131072
